TPU v7x, 256 devices: a whole 4x4x8 slice. The times are simulated.
256 devices in a mesh: outer: 64 (over x_hi, z, y), inner: 4 (over x_lo, core).
Axes of the slice: x: 4 (x_hi: 2, x_lo: 2; x = x_hi * 2 + x_lo), y: 4, z: 8, core: 2. Of those that a mesh axis runs over, the one named last changes fastest.
Arguments:
- queries: bfloat16 [65536, 1536], P(('outer', 'inner')), may hold values from -8 to 8
- key_rows: bfloat16 [65536, 1536], P(('outer', 'inner')), may hold values from -8 to 8
- value_rows: bfloat16 [65536, 1536], P(('outer', 'inner')), may hold values from -6 to 6
- upstream: bfloat16 [65536, 1536], P(('outer', 'inner')), may hold values from -6 to 6
- short_offsets: int32 [16], replicated, may hold values from 0 to 1
- global_offsets: int32 [16], replicated, may hold values from 0 to 127
Outputs:
- grad_queries: bfloat16 [65536, 1536], P(('outer', 'inner'))
- grad_keys: bfloat16 [65536, 1536], P(('outer', 'inner'))
- grad_values: bfloat16 [65536, 1536], P(('outer', 'inner'))
All inputs are finite; a program needn't handle non-finite values.
Results may differ from a plain program's by a relative error of at most 0.006.
The roundings to bfloat16 on the way count: a program that leaves them out, or rounds other values in their place, can miss the bound.
Values may be sent and summed in bfloat16 or wider, within the bound.
No kernel may reach another device: no remote copies, remote signals or barrier semaphores. Data moves between devices by JAX's collectives and lax.ppermute only.
A program may use at most 128 MiB of HBM per device.

v0:
```python
import jax
import jax.numpy as jnp
from jax import lax
from jax.sharding import PartitionSpec as P

H = 16
HD = 96
D = 1536
TOK_DEV = 256
KEEP_A = 512
KEEP_B = 512


def pick_rows(block, offsets, stride):
    count = block.shape[0] // stride
    shaped = block.reshape(count, stride, H, HD)
    onehot = (jnp.arange(stride, dtype=jnp.int32)[:, None] == offsets[None, :]).astype(block.dtype)
    return jnp.sum(shaped * onehot[None, :, :, None], axis=1)


def put_rows(grads, offsets, stride):
    onehot = (jnp.arange(stride, dtype=jnp.int32)[:, None] == offsets[None, :]).astype(jnp.float32)
    spread = grads[:, None, :, :] * onehot[None, :, :, None]
    return spread.reshape(grads.shape[0] * stride, H * HD)


def as_heads(flat):
    return flat.reshape(flat.shape[0], H, HD)


def attend_back(query_part, key_part, value_part, grad_part):
    softmax_scale = HD ** (-0.5)
    scores = (
        jnp.einsum("qhd,khd->hqk", query_part, key_part, preferred_element_type=jnp.float32)
        * softmax_scale
    )
    row_max = jnp.max(scores, axis=-1, keepdims=True)
    weights = jnp.exp(scores - row_max)
    probs = weights / jnp.sum(weights, axis=-1, keepdims=True)
    probs_low = probs.astype(jnp.bfloat16)
    output = jnp.einsum("hqk,khd->qhd", probs_low, value_part, preferred_element_type=jnp.float32)
    delta = jnp.sum(grad_part.astype(jnp.float32) * output, axis=-1)
    dprobs = jnp.einsum("qhd,khd->hqk", grad_part, value_part, preferred_element_type=jnp.float32)
    dscores = (probs * (dprobs - jnp.transpose(delta)[:, :, None])).astype(jnp.bfloat16)
    grad_q = (
        jnp.einsum("hqk,khd->qhd", dscores, key_part, preferred_element_type=jnp.float32)
        * softmax_scale
    )
    grad_k = (
        jnp.einsum("hqk,qhd->khd", dscores, query_part, preferred_element_type=jnp.float32)
        * softmax_scale
    )
    grad_v = jnp.einsum("hqk,qhd->khd", probs_low, grad_part, preferred_element_type=jnp.float32)
    return (grad_q, grad_k, grad_v)


def grouped_back(query_part, key_part, value_part, grad_part):
    head_groups = 4

    def split_heads(member):
        return jnp.moveaxis(
            member.reshape(member.shape[0], head_groups, H // head_groups, HD), 1, 0
        )

    def single_group(pack):
        return attend_back(pack[0], pack[1], pack[2], pack[3])

    mapped = lax.map(
        single_group,
        (
            split_heads(query_part),
            split_heads(key_part),
            split_heads(value_part),
            split_heads(grad_part),
        ),
    )
    return [jnp.moveaxis(member, 0, 1).reshape(member.shape[1], H, HD) for member in mapped]


def local(queries, key_rows, value_rows, upstream, short_offsets, global_offsets):
    inner_size = lax.axis_size("inner")
    all_size = lax.axis_size(("outer", "inner"))
    short_stride = TOK_DEV * inner_size // KEEP_A
    far_count = KEEP_B // all_size
    far_stride = TOK_DEV // far_count
    near = [
        pick_rows(member, short_offsets, short_stride)
        for member in (queries, key_rows, value_rows, upstream)
    ]
    near_count = near[0].shape[0]
    segment_keys, segment_values = (
        lax.all_gather(near[1].reshape(near_count, D), "inner", axis=0, tiled=True),
        lax.all_gather(near[2].reshape(near_count, D), "inner", axis=0, tiled=True),
    )
    near_grads = attend_back(near[0], as_heads(segment_keys), as_heads(segment_values), near[3])
    returned = (
        lax.psum_scatter(
            near_grads[1].reshape(KEEP_A, D), "inner", scatter_dimension=0, tiled=True
        ),
        lax.psum_scatter(
            near_grads[2].reshape(KEEP_A, D), "inner", scatter_dimension=0, tiled=True
        ),
    )
    near_final = [near_grads[0], as_heads(returned[0]), as_heads(returned[1])]
    far = [
        pick_rows(member, global_offsets, far_stride).reshape(far_count, D)
        for member in (queries, key_rows, value_rows, upstream)
    ]
    gathered = (
        lax.all_gather(far[0], ("outer", "inner"), axis=0, tiled=True),
        lax.all_gather(far[1], ("outer", "inner"), axis=0, tiled=True),
        lax.all_gather(far[2], ("outer", "inner"), axis=0, tiled=True),
        lax.all_gather(far[3], ("outer", "inner"), axis=0, tiled=True),
    )
    whole_grads = grouped_back(
        as_heads(gathered[0]), as_heads(gathered[1]), as_heads(gathered[2]), as_heads(gathered[3])
    )
    start = lax.axis_index(("outer", "inner")) * far_count
    far_final = [lax.dynamic_slice_in_dim(member, start, far_count, 0) for member in whole_grads]
    results = []
    for index in range(3):
        total = put_rows(near_final[index], short_offsets, short_stride) + put_rows(
            far_final[index], global_offsets, far_stride
        )
        results.append(total.astype(jnp.bfloat16))
    return (results[0], results[1], results[2])


def solution(mesh):
    in_specs = (
        P(("outer", "inner"), None),
        P(("outer", "inner"), None),
        P(("outer", "inner"), None),
        P(("outer", "inner"), None),
        P(),
        P(),
    )
    out_specs = (
        P(("outer", "inner"), None),
        P(("outer", "inner"), None),
        P(("outer", "inner"), None),
    )
    return jax.shard_map(local, mesh=mesh, in_specs=in_specs, out_specs=out_specs, check_vma=False)
```

profile of v0, /device:TPU:32, one launch (start us, length us, event | category | flops | bytes accessed | tf_op | source)
XLA Modules:
  0.0 1869.0 jit_solution(2609448415388892153)
XLA Ops:
  15.6 4.7 multiply_reduce_fusion.4
  33.9 8.9 multiply_reduce_fusion.6
  51.6 4.9 fusion.81
  59.1 22.5 %all-gather.13.cloned.1.call-done = bf16[512,1536]{0,1:T(8,128)(2,1)} async-done(((bf16[128,1536]{0,1:T(8,128)(2,1)}), bf16[512,1536]{0,1:T(8,128)(2,1)}) %all-gather.13.cloned.1.call-update) | async-done | bytes 1572880 | tf_op jit(solution)/shard_map/all_gather | solution.py:93
  89.1 3.7 fusion.62
  97.6 405.1 %all-gather.15.cloned.1.call-done = bf16[256,2,1536]{2,1,0:T(2,128)(2,1)} async-done(((bf16[1,2,1536]{2,1,0:T(2,128)(2,1)}), bf16[256,2,1536]{2,1,0:T(2,128)(2,1)}) %all-gather.15.cloned.1.call-update) | async-done | bytes 1572880 | tf_op jit(solution)/shard_map/all_gather | solution.py:111
  502.7 5.2 reshape_reshape.12
  510.8 407.4 %all-gather.19.cloned.1.call-done = bf16[256,2,1536]{2,1,0:T(2,128)(2,1)} async-done(((bf16[1,2,1536]{2,1,0:T(2,128)(2,1)}), bf16[256,2,1536]{2,1,0:T(2,128)(2,1)}) %all-gather.19.cloned.1.call-update) | async-done | bytes 1572880 | tf_op jit(solution)/shard_map/all_gather | solution.py:113
  918.2 5.8 reshape_reshape.14
  926.9 406.7 %all-gather.21.cloned.1.call-done = bf16[256,2,1536]{2,1,0:T(2,128)(2,1)} async-done(((bf16[1,2,1536]{2,1,0:T(2,128)(2,1)}), bf16[256,2,1536]{2,1,0:T(2,128)(2,1)}) %all-gather.21.cloned.1.call-update) | async-done | bytes 1572880 | tf_op jit(solution)/shard_map/all_gather | solution.py:112
  1333.6 5.8 reshape_reshape.15
  1339.5 4.2 copy.91
  1343.6 406.1 %all-gather.17.cloned.1.call-done = bf16[256,2,1536]{2,1,0:T(2,128)(2,1)} async-done(((bf16[1,2,1536]{2,1,0:T(2,128)(2,1)}), bf16[256,2,1536]{2,1,0:T(2,128)(2,1)}) %all-gather.17.cloned.1.call-update) | async-done | bytes 1572880 | tf_op jit(solution)/shard_map/all_gather | solution.py:110
  1749.7 5.8 reshape_reshape.13
  1755.5 4.3 copy.89
  1759.8 60.5 %while.14 = (s32[]{:T(128)}, f32[4,512,4,96]{1,3,2,0:T(8,128)}, f32[4,512,4,96]{1,3,2,0:T(8,128)}, f32[4,512,4,96]{1,3,2,0:T(8,128)}, bf16[4,512,4,96]{1,3,2,0:T...) while((s32[]{:T(128)}, f32[4,512,4,96]{1,3,2,0:T(8,128)}, ...), condition=%wide.region_15.0_spmd, body=%wide.region_11.15_spmd.sunk | while | flops 1218378240 | bytes 54179996 | solution.py:68
  1759.8 4.7 fusion.131
  1775.0 4.5 fusion.131
  1790.1 4.5 fusion.131
  1805.0 4.5 fusion.131
  1823.5 7.4 broadcast_multiply_fusion.3
  1842.7 4.6 broadcast_multiply_fusion
  1847.3 3.1 mul.247
  1855.6 3.1 add_convert_fusion
  (142 shorter events, 116.6 us)
Async XLA Ops:
  7.2 44.5 %all-gather.11.cloned.1.call-start = ((), (), s32[]{:S(2)}) async-start(), calls=%async_computation.2 | async-start | bytes 1966080 | tf_op jit(solution)/shard_map/all_gather | solution.py:92
  20.3 5.2 copy-start.9
  20.3 6.4 copy-start.11
  22.7 58.9 %all-gather.13.cloned.1.call-start = ((), (), s32[]{:S(2)}) async-start(), calls=%async_computation.3 | async-start | bytes 1966080 | tf_op jit(solution)/shard_map/all_gather | solution.py:93
  22.7 5.2 copy-start.12
  25.0 3.1 copy-start.13
  25.1 477.6 %all-gather.15.cloned.1.call-start = ((), (), s32[]{:S(2)}) async-start(), calls=%async_computation.6 | async-start | bytes 1579008 | tf_op jit(solution)/shard_map/all_gather | solution.py:111
  30.5 3.2 copy-start.19
  42.8 7.9 copy-start.17
  44.6 873.5 %all-gather.19.cloned.1.call-start = ((), (), s32[]{:S(2)}) async-start(), calls=%async_computation.8 | async-start | bytes 1579008 | tf_op jit(solution)/shard_map/all_gather | solution.py:113
  46.5 1287.1 %all-gather.21.cloned.1.call-start = ((), (), s32[]{:S(2)}) async-start(), calls=%async_computation.9 | async-start | bytes 1579008 | tf_op jit(solution)/shard_map/all_gather | solution.py:112
  48.3 1701.3 %all-gather.17.cloned.1.call-start = ((), (), s32[]{:S(2)}) async-start(), calls=%async_computation.7 | async-start | bytes 1579008 | tf_op jit(solution)/shard_map/all_gather | solution.py:110
  49.2 1788.4 %reduce-scatter.3.cloned.1.call-start = ((), (), s32[]{:S(2)}) async-start(), calls=%async_computation.4 | async-start | bytes 3932160 | tf_op jit(solution)/shard_map/reduce_scatter | solution.py:97
  89.0 1751.2 %reduce-scatter.5.cloned.1.call-start = ((), (), s32[]{:S(2)}) async-start(), calls=%async_computation.5 | async-start | bytes 3932160 | tf_op jit(solution)/shard_map/reduce_scatter | solution.py:100
  1755.5 4.3 copy-start.2
  1764.4 3.0 copy-start.3
  1764.4 4.1 copy-start
  1779.6 4.0 copy-start
  1794.6 3.9 copy-start
  1809.5 3.0 copy-start.3
  1809.5 4.1 copy-start
  1837.6 5.1 copy-start.8
  1855.6 3.1 copy-start.4
  1855.6 3.1 copy-start.6
  (10 other events, 23.0 us)
Sparse Core Ops, SparseCore 0:
  22.8 28.7 all-gather.10
  53.4 28.0 all-gather.12
  84.0 418.6 all-gather.14
  504.4 413.6 all-gather.18
  919.9 413.6 all-gather.20
  1335.9 413.6 all-gather.16
  1752.2 36.1 reduce-scatter.2
  1791.0 40.2 reduce-scatter.4
where the time goes:
time: 1880 us; the launch traced here: 1870 us
  waiting for transfers between devices  1650 us (88%)
  local copies, waits for them, and re-layouts  94.6 us (5%)
  matrix products  64.3 us (3%)
  other arithmetic  46.1 us (2%)
    all_gather x1, waiting for transfers between devices, local(): lax.all_gather(far[3], ('outer', 'inner'), axis=0, tiled=True)  407 us
    all_gather x1, waiting for transfers between devices, local(): lax.all_gather(far[2], ('outer', 'inner'), axis=0, tiled=True)  407 us
    all_gather x1, waiting for transfers between devices, local(): lax.all_gather(far[0], ('outer', 'inner'), axis=0, tiled=True)  406 us
    all_gather x1, waiting for transfers between devices, local(): lax.all_gather(far[1], ('outer', 'inner'), axis=0, tiled=True)  405 us
  transfers between devices with their start and end apart: 8, of which 6 were waited for; matrix products, arithmetic and copies ran while one was open for 9% of the time, Pallas kernels for 0%

commit v1 on v0

--- a/solution.py
+++ b/solution.py
@@ -107,7 +107,12 @@
         for member in (queries, key_rows, value_rows, upstream)
     ]
     gathered = (
-        lax.all_gather(far[0], ("outer", "inner"), axis=0, tiled=True),
+        jnp.concatenate(
+            lax.all_to_all(
+                jnp.stack([far[0]] * lax.axis_size(("outer", "inner"))), ("outer", "inner"), 0, 0
+            ),
+            axis=0,
+        ),
         lax.all_gather(far[1], ("outer", "inner"), axis=0, tiled=True),
         lax.all_gather(far[2], ("outer", "inner"), axis=0, tiled=True),
         lax.all_gather(far[3], ("outer", "inner"), axis=0, tiled=True),

time: 1880 us -> 1480 us (0.79)
  waiting for transfers between devices: 1650 us -> 1230 us
    all_gather x1 -> x0, waiting for transfers between devices: 406 us -> none  [local(): lax.all_gather(far[0], ('outer', 'inner'), axis=0, tiled=True)]
  transfers between devices with their start and end apart: 8 -> 8, of which waited for: 6 -> 5; matrix products, arithmetic and copies ran while one was open for 9% -> 11% of each run, Pallas kernels for 0% -> 0%
where the time goes in v1:
time: 1480 us; the launch traced here: 1470 us
  waiting for transfers between devices  1230 us (83%)
  local copies, waits for them, and re-layouts  96.1 us (6%)
  matrix products  64.1 us (4%)
  other arithmetic  46 us (3%)
  starting transfers between devices  15.3 us (1%)
    all_gather x1, waiting for transfers between devices, local(): lax.all_gather(far[3], ('outer', 'inner'), axis=0, tiled=True)  413 us
    all_gather x1, waiting for transfers between devices, local(): lax.all_gather(far[2], ('outer', 'inner'), axis=0, tiled=True)  407 us
    all_gather x1, waiting for transfers between devices, local(): lax.all_gather(far[1], ('outer', 'inner'), axis=0, tiled=True)  390 us
  transfers between devices with their start and end apart: 8, of which 5 were waited for; matrix products, arithmetic and copies ran while one was open for 11% of the time, Pallas kernels for 0%

profile of v1, /device:TPU:32, one launch (start us, length us, event | category | flops | bytes accessed | tf_op | source)
XLA Modules:
  0.0 1470.9 jit_solution(6040266071188233892)
XLA Ops:
  15.6 4.7 multiply_reduce_fusion.4
  33.9 8.9 multiply_reduce_fusion.6
  51.6 4.9 fusion.81
  59.1 22.5 %all-gather.11.cloned.1.call-done = bf16[512,1536]{0,1:T(8,128)(2,1)} async-done(((bf16[128,1536]{0,1:T(8,128)(2,1)}), bf16[512,1536]{0,1:T(8,128)(2,1)}) %all-gather.11.cloned.1.call-update) | async-done | bytes 1572880 | tf_op jit(solution)/shard_map/all_gather | solution.py:93
  91.2 14.5 all-to-all-start
  105.8 3.7 fusion.62
  114.4 390.1 %all-gather.13.cloned.1.call-done = bf16[256,2,1536]{2,1,0:T(2,128)(2,1)} async-done(((bf16[1,2,1536]{2,1,0:T(2,128)(2,1)}), bf16[256,2,1536]{2,1,0:T(2,128)(2,1)}) %all-gather.13.cloned.1.call-update) | async-done | bytes 1572880 | tf_op jit(solution)/shard_map/all_gather | solution.py:116
  504.5 5.2 reshape_reshape.9
  512.6 413.4 %all-gather.15.cloned.1.call-done = bf16[256,2,1536]{2,1,0:T(2,128)(2,1)} async-done(((bf16[1,2,1536]{2,1,0:T(2,128)(2,1)}), bf16[256,2,1536]{2,1,0:T(2,128)(2,1)}) %all-gather.15.cloned.1.call-update) | async-done | bytes 1572880 | tf_op jit(solution)/shard_map/all_gather | solution.py:118
  925.9 5.8 reshape_reshape.10
  934.7 407.2 %all-gather.17.cloned.1.call-done = bf16[256,2,1536]{2,1,0:T(2,128)(2,1)} async-done(((bf16[1,2,1536]{2,1,0:T(2,128)(2,1)}), bf16[256,2,1536]{2,1,0:T(2,128)(2,1)}) %all-gather.17.cloned.1.call-update) | async-done | bytes 1572880 | tf_op jit(solution)/shard_map/all_gather | solution.py:117
  1342.0 5.8 reshape_reshape.11
  1347.8 4.2 copy.91
  1352.0 6.0 reshape_reshape_reshape.3
  1358.0 4.3 copy.89
  1362.2 60.1 %while.14 = (s32[]{:T(128)}, f32[4,512,4,96]{1,3,2,0:T(8,128)}, f32[4,512,4,96]{1,3,2,0:T(8,128)}, f32[4,512,4,96]{1,3,2,0:T(8,128)}, bf16[4,512,4,96]{1,3,2,0:T...) while((s32[]{:T(128)}, f32[4,512,4,96]{1,3,2,0:T(8,128)}, ...), condition=%wide.region_15.0_spmd, body=%wide.region_11.15_spmd.sunk | while | flops 1218378240 | bytes 54179996 | solution.py:68
  1362.2 4.5 fusion.131
  1377.3 4.5 fusion.131
  1392.2 4.5 fusion.131
  1407.1 4.5 fusion.131
  1425.6 7.2 broadcast_multiply_fusion.3
  1444.6 4.6 broadcast_multiply_fusion
  1449.2 3.1 mul.247
  1457.5 3.1 add_convert_fusion
  (142 shorter events, 118.6 us)
Async XLA Ops:
  7.2 44.4 %all-gather.9.cloned.1.call-start = ((), (), s32[]{:S(2)}) async-start(), calls=%async_computation.3 | async-start | bytes 1966080 | tf_op jit(solution)/shard_map/all_gather | solution.py:92
  20.3 5.2 copy-start.9
  20.3 6.4 copy-start.11
  22.7 58.9 %all-gather.11.cloned.1.call-start = ((), (), s32[]{:S(2)}) async-start(), calls=%async_computation.4 | async-start | bytes 1966080 | tf_op jit(solution)/shard_map/all_gather | solution.py:93
  22.7 5.2 copy-start.12
  25.0 3.1 copy-start.13
  25.1 479.4 %all-gather.13.cloned.1.call-start = ((), (), s32[]{:S(2)}) async-start(), calls=%async_computation.7 | async-start | bytes 1579008 | tf_op jit(solution)/shard_map/all_gather | solution.py:116
  30.5 3.2 copy-start.19
  42.8 7.1 copy-start.17
  44.6 881.3 %all-gather.15.cloned.1.call-start = ((), (), s32[]{:S(2)}) async-start(), calls=%async_computation.8 | async-start | bytes 1579008 | tf_op jit(solution)/shard_map/all_gather | solution.py:118
  46.5 1295.5 %all-gather.17.cloned.1.call-start = ((), (), s32[]{:S(2)}) async-start(), calls=%async_computation.9 | async-start | bytes 1579008 | tf_op jit(solution)/shard_map/all_gather | solution.py:117
  48.3 1391.1 %reduce-scatter.3.cloned.1.call-start = ((), (), s32[]{:S(2)}) async-start(), calls=%async_computation.5 | async-start | bytes 3932160 | tf_op jit(solution)/shard_map/reduce_scatter | solution.py:97
  91.2 1260.8 %all-to-all-start = ((bf16[256,2,1536]{2,1,0:T(2,128)(2,1)}), bf16[256,2,1536]{2,1,0:T(2,128)(2,1)}, u32[]{:S(2)}, u32[]{:S(2)}) async-start(bf16[256,2,1536]{2,1,0:T(2,128)(2,1)} %stack.3), calls=%async_computation | async-start | bytes 3145728 | tf_op jit(solution)/shard_map/all_to_all | solution.py:111
  105.7 1336.3 %reduce-scatter.5.cloned.1.call-start = ((), (), s32[]{:S(2)}) async-start(), calls=%async_computation.6 | async-start | bytes 3932160 | tf_op jit(solution)/shard_map/reduce_scatter | solution.py:100
  1358.0 4.3 copy-start.2
  1366.7 3.0 copy-start.3
  1366.7 4.0 copy-start
  1381.8 3.9 copy-start
  1396.7 3.9 copy-start
  1411.6 3.0 copy-start.3
  1411.6 4.0 copy-start
  1439.5 5.2 copy-start.8
  1457.5 3.1 copy-start.4
  1457.5 3.1 copy-start.6
  (10 other events, 23.0 us)
Sparse Core Ops, SparseCore 0:
  22.8 28.7 all-gather.8
  53.4 28.0 all-gather.10
  84.0 420.4 all-gather.12
  506.2 419.6 all-gather.14
  928.2 413.6 all-gather.16
  1344.4 36.1 reduce-scatter.2
  1383.2 40.2 reduce-scatter.4
